TPU v7x, 32 devices: a whole 2x2x4 slice. The times are simulated.
32 devices in a mesh: group: 2 (over x), fsdp: 8 (over z, y), ctx: 2 (over core).
Axes of the slice: x: 2, y: 2, z: 4, core: 2. Of those that a mesh axis runs over, the one named last changes fastest.
Arguments:
- normed: bfloat16 [16, 512, 8192], P(('group', 'fsdp'), 'ctx'), parts along dimension 0, may hold values from -6 to 6
- queries: bfloat16 [16, 512, 4096], P(('group', 'fsdp'), 'ctx'), parts along dimension 0, may hold values from -103 to 103
- key_weight: bfloat16 [8192, 512], P('fsdp'), may hold values from -0.0625 to 0.0625
- value_weight: bfloat16 [8192, 512], P('fsdp'), may hold values from -0.0625 to 0.0625
- doc_start: int32 [16], P(('group', 'fsdp')), parts along dimension 0, may hold values from 1 to 511
Outputs:
- attention: bfloat16 [16, 512, 4096], P(('group', 'fsdp'), 'ctx'), parts along dimension 0
There are 2 independent parts, one for each index of `group`. A program takes and returns all parts, laid end to end along the dimension named above; an argument that names none is the same for every part. Nothing has to cross between parts.
Inputs may be any that keep to these rules, and one draw needn't show every extreme that they name: Rows before doc_start of a window belong to one document and the other rows to the next.
All inputs are finite; a program needn't handle non-finite values.
Results may differ from a plain program's by a relative error of at most 0.0055.
The roundings to bfloat16 on the way count: a program that leaves them out, or rounds other values in their place, can miss the bound.
Values may be sent and summed in bfloat16 or wider, within the bound.
A program may use at most 128 MiB of HBM per device.

v0:
```python
import jax
import jax.numpy as jnp
from jax import lax
from jax.sharding import PartitionSpec as P

HEAD_DIM = 128
GROUP = 8


theta_base = 500000.0
masked_score = -1e30


def rotate(values, positions):
    head_width = values.shape[-1]
    half_width = head_width // 2
    frequency = theta_base ** (-jnp.arange(half_width, dtype=jnp.float32) * 2.0 / head_width)
    angles = positions.astype(jnp.float32)[:, None] * frequency[None, :]
    cosine = jnp.cos(angles)[:, None, :]
    sine_part = jnp.sin(angles)[:, None, :]
    first_half = values[..., :half_width]
    second_half = values[..., half_width:]
    return jnp.concatenate(
        [
            first_half * cosine - second_half * sine_part,
            second_half * cosine + first_half * sine_part,
        ],
        axis=-1,
    )


def keep_state(carry_state):
    return carry_state


def attend(carry_state, query_block, positions, doc_bound, key_block, value_block, key_start):
    key_count = key_block.shape[1]
    key_rows = jnp.arange(key_count, dtype=jnp.int32)
    score_scale = query_block.shape[-1] ** (-0.5)

    def compute_block(old_state):
        running_max, denominator, summed = old_state
        scores = (
            jnp.einsum(
                "wrkgd,wskd->wkgrs", query_block, key_block, preferred_element_type=jnp.float32
            )
            * score_scale
        )
        before_query = key_rows[None, None, :] <= positions[None, :, None]
        same_document = (key_rows[None, None, :] >= doc_bound[:, None, None]) | (
            positions[None, :, None] < doc_bound[:, None, None]
        )
        visible = (before_query & same_document)[:, None, None, :, :]
        scores = jnp.where(visible, scores, masked_score)
        new_max = jnp.maximum(running_max, jnp.max(scores, axis=-1))
        weights = jnp.where(visible, jnp.exp(scores - new_max[..., None]), 0.0)
        denominator = jnp.sum(weights, axis=-1)
        summed = jnp.einsum(
            "wkgrs,wskd->wkgrd",
            weights.astype(jnp.bfloat16),
            value_block,
            preferred_element_type=jnp.float32,
        )
        return (new_max, denominator, summed)

    return lax.cond(key_start > jnp.max(positions), keep_state, compute_block, carry_state)


def body(normed, queries, key_weight, value_weight, doc_start):
    windows, block_rows, model_width = normed.shape
    flattened = normed.reshape(windows * block_rows, model_width)
    kv_width = key_weight.shape[1]
    kv_heads = kv_width // HEAD_DIM
    pieces = (
        lax.all_gather(key_weight, "fsdp", axis=0, tiled=True),
        lax.all_gather(value_weight, "fsdp", axis=0, tiled=True),
    )
    key_proj = jnp.dot(flattened, pieces[0], preferred_element_type=jnp.float32)
    value_proj = jnp.dot(flattened, pieces[1], preferred_element_type=jnp.float32)
    cycle_index = lax.axis_index("ctx")
    own_rows = cycle_index * block_rows + jnp.arange(block_rows, dtype=jnp.int32)
    key_heads = rotate(key_proj.reshape(windows, block_rows, kv_heads, HEAD_DIM), own_rows).astype(
        jnp.bfloat16
    )
    value_heads = value_proj.astype(jnp.bfloat16).reshape(windows, block_rows, kv_heads, HEAD_DIM)
    query_heads = rotate(
        queries.astype(jnp.float32).reshape(windows, block_rows, kv_heads * GROUP, HEAD_DIM),
        own_rows,
    )
    query_heads = query_heads.astype(jnp.bfloat16).reshape(
        windows, block_rows, kv_heads, GROUP, HEAD_DIM
    )
    query_groups = ((query_heads, own_rows),)

    def initial_state(query_group):
        group_rows = query_group[1].shape[0]
        return (
            jnp.full((windows, kv_heads, GROUP, group_rows), masked_score, jnp.float32),
            jnp.zeros((windows, kv_heads, GROUP, group_rows), jnp.float32),
            jnp.zeros((windows, kv_heads, GROUP, group_rows, HEAD_DIM), jnp.float32),
        )

    def add_block(states, pieces, row_start):
        return tuple(
            (
                attend(
                    carry_state,
                    query_group[0],
                    query_group[1],
                    doc_start,
                    pieces[0],
                    pieces[1],
                    row_start,
                )
                for carry_state, query_group in zip(states, query_groups)
            )
        )

    states = add_block(
        tuple((initial_state(query_group) for query_group in query_groups)),
        (
            lax.all_gather(key_heads, "ctx", axis=1, tiled=True),
            lax.all_gather(value_heads, "ctx", axis=1, tiled=True),
        ),
        jnp.int32(0),
    )

    def finish(carry_state):
        running_max, denominator, summed = carry_state
        context = summed / denominator[..., None]
        group_rows = context.shape[3]
        return (
            jnp.transpose(context, (0, 3, 1, 2, 4))
            .astype(jnp.bfloat16)
            .reshape(windows, group_rows, kv_heads * GROUP * HEAD_DIM)
        )

    outputs = [finish(carry_state) for carry_state in states]
    return outputs[0]


def solution(mesh):
    placed = (
        P(("group", "fsdp"), "ctx", None),
        P(("group", "fsdp"), "ctx", None),
        P("fsdp", None),
        P("fsdp", None),
        P(("group", "fsdp")),
    )
    return jax.shard_map(
        body,
        mesh=mesh,
        in_specs=placed,
        out_specs=P(("group", "fsdp"), "ctx", None),
        check_vma=False,
    )
```

profile of v0, /device:TPU:0, one launch (start us, length us, event | category | flops | bytes accessed | tf_op | source)
XLA Modules:
  0.0 313.6 jit_solution(7447207940935423399)
XLA Ops:
  6.5 0.0 all-gather.3.cloned.1.call-start
  6.5 0.7 all-gather.3.cloned.1.call-update
  7.3 0.0 all-gather.5.cloned.1.call-start
  7.3 0.7 all-gather.5.cloned.1.call-update
  8.0 0.6 fusion.28
  9.3 0.3 multiply_cosine_fusion
  9.6 0.1 copy.10
  9.7 0.1 copy.12
  9.8 2.1 convert_bitcast_fusion
  11.9 0.8 copy.21
  12.7 1.5 fusion.30
  14.2 4.9 %subtract_convert_fusion = (bf16[1,256,32,64]{3,1,2,0:T(8,128)(2,1)S(1)}, bf16[1,256,32,64]{3,1,2,0:T(8,128)(2,1)S(1)}) fusion(f32[1,256,32,64]{3,2,1,0:T(8,128)S(1)} %get-tuple-element.43, f32[1,256,32,64]{3,2,1,0:T(8,128)S(1)} %get-tuple-element.42, f32[256,64]{1,0:T(8,128)S(1)} %copy.12, f32[256,64]{1,0:T(8,128)S(1)} %copy.10), kind=kLoop, calls=%fused_computation.27 | loop fusion | flops 4194304 | bytes 6422528 | tf_op jit(solution)/shard_map/convert.4
  19.1 1.2 pad_maximum_fusion
  20.2 116.5 %all-gather.3.cloned.1.call-done = bf16[8192,512]{1,0:T(8,128)(2,1)} async-done(((bf16[1024,512]{1,0:T(8,128)(2,1)}), bf16[8192,512]{1,0:T(8,128)(2,1)}) %all-gather.3.cloned.1.call-update) | async-done | bytes 8388624 | tf_op jit(solution)/shard_map/all_gather | solution.py:75
  136.7 12.1 %copy.8 = bf16[512,8192]{1,0:T(8,128)(2,1)} copy(bf16[512,8192]{0,1:T(8,128)(2,1)} %bitcast.77) | data formatting | bytes 16777216 | tf_op jit(solution)/shard_map/dot_general | solution.py:78
  148.8 7.0 %fusion.22 = f32[1,256,4,128]{1,3,2,0:T(8,128)S(1)} fusion(bf16[4,128,8192]{2,1,0:T(8,128)(2,1)} %bitcast.78, bf16[1,256,8192]{2,1,0:T(8,128)(2,1)} %param.7), kind=kOutput, calls=%fused_computation.30 | convolution fusion | flops 2147483648 | bytes 13107200 | tf_op jit(solution)/shard_map/dot_general | solution.py:78
  155.9 105.6 %all-gather.5.cloned.1.call-done = bf16[8192,512]{1,0:T(8,128)(2,1)} async-done(((bf16[1024,512]{1,0:T(8,128)(2,1)}), bf16[8192,512]{1,0:T(8,128)(2,1)}) %all-gather.5.cloned.1.call-update) | async-done | bytes 8388624 | tf_op jit(solution)/shard_map/all_gather | solution.py:76
  261.5 7.0 %fusion.25 = bf16[256,512]{1,0:T(8,128)(2,1)S(1)} fusion(bf16[8192,512]{1,0:T(8,128)(2,1)} %all-gather.5.cloned.1.call-done, bf16[1,256,8192]{2,1,0:T(8,128)(2,1)} %param.7), kind=kOutput, calls=%fused_computation.31 | convolution fusion | flops 2147614720 | bytes 12845056 | tf_op jit(solution)/shard_map/dot_general | solution.py:79
  268.5 0.1 reshape.279
  268.6 0.1 subtract_convert_fusion.1
  268.7 2.2 all_gather.13
  270.9 2.2 all_gather.15
  273.1 27.1 %conditional.1 = (f32[1,4,8,256]{3,2,1,0:T(8,128)S(1)}, f32[1,4,8,256,128]{4,3,2,1,0:T(8,128)}) conditional(s32[]{:T(128)} %convert_element_type.43, (s32[512]{0:T(512)S(1)}, s32[256]{0:T(256)S(1)}, s32[1]{0:T(128)}, s32[512]{0:T(512)S(1)}, bf16[1,512,4,128]{1,3,2,0:T(8,128)(2,1)S(1)}, /*index=5*/bf16[1,256,4,8,128]{4,1,3,2,0:T(8,128)(2,1)S(1)}, ...), branch_computations={%region_1.4_spmd, %region_4.5_spmd} | conditional | flops 2202395392 | bytes 125509176 | solution.py:66
  273.1 0.6 broadcast_compare_fusion
  273.7 0.7 broadcast_compare_fusion.1
  274.4 0.2 or_and_fusion
  274.6 2.8 fusion
  277.4 0.0 copy-start
  277.4 5.7 %copy-done = f32[4,512,256,8]{2,1,3,0:T(8,128)} copy-done((f32[4,512,256,8]{2,1,3,0:T(8,128)}, f32[4,512,256,8]{2,1,3,0:T(8,128)S(1)}, u32[]{:S(2)}) %copy-start) | copy-done | bytes 16777240 | tf_op jit(solution)/shard_map/cond
  283.1 4.2 %fusion.2 = f32[4,8,256]{2,1,0:T(8,128)S(1)} fusion(f32[4,512,256,8]{2,1,3,0:T(8,128)S(1)} %get-tuple-element.39, f32[4,8,256]{2,1,0:T(8,128)S(1)} %broadcast_maximum_fusion, pred[256,512]{0,1:T(8,128)(4,1)S(1)} %or_and_fusion), kind=kLoop, calls=%fused_computation.4 | loop fusion | flops 20963328 | bytes 16973824 | tf_op jit(solution)/shard_map/cond/branch_0_fun/reduce_sum | solution.py:57
  287.3 12.9 %fusion.7 = f32[1,4,8,256,128]{4,3,2,1,0:T(8,128)} fusion(f32[4,512,256,8]{2,1,3,0:T(8,128)} %copy-done, f32[4,8,256]{2,1,0:T(8,128)S(1)} %broadcast_maximum_fusion, pred[256,512]{0,1:T(8,128)(4,1)S(1)} %or_and_fusion, bf16[1,512,4,128]{3,1,2,0:T(8,128)(2,1)S(1)} %get-tuple-element.24), kind=kOutput, calls=%fused_computation.8 | convolution fusion | flops 1094713344 | bytes 21659648 | tf_op jit(solution)/shard_map/cond/branch_0_fun/wkgrs,wskd->wkgrd/dot_general | solution.py:58
  300.2 2.9 fusion.21
  303.1 1.4 copy.15
  304.4 2.3 reshape.280
  (6 shorter events, 0.1 us)
Async XLA Ops:
  6.5 130.2 %all-gather.3.cloned.1.call-start = ((), (), s32[]{:S(2)}) async-start(), calls=%async_computation | async-start | bytes 9437184 | tf_op jit(solution)/shard_map/all_gather | solution.py:75
  7.3 254.2 %all-gather.5.cloned.1.call-start = ((), (), s32[]{:S(2)}) async-start(), calls=%async_computation.1 | async-start | bytes 9437184 | tf_op jit(solution)/shard_map/all_gather | solution.py:76
  277.4 5.7 %copy-start = (f32[4,512,256,8]{2,1,3,0:T(8,128)}, f32[4,512,256,8]{2,1,3,0:T(8,128)S(1)}, u32[]{:S(2)}) copy-start(f32[4,512,256,8]{2,1,3,0:T(8,128)S(1)} %get-tuple-element.39) | copy-start | bytes 50331652 | tf_op jit(solution)/shard_map/cond
Sparse Core Ops, SparseCore 0:
  9.5 127.1 all-gather.2
  138.8 122.6 all-gather.4
where the time goes:
time: 314 us
  waiting for transfers between devices  224 us (71%)
  matrix products  29.7 us (9%)
  local copies, waits for them, and re-layouts  24 us (8%)
  other arithmetic  17.7 us (6%)
  between operations  14.2 us (5%)
  blocking collectives  4.35 us (1%)
    all_gather x1, waiting for transfers between devices, body(): lax.all_gather(key_weight, 'fsdp', axis=0, tiled=True)  116 us
    all_gather x1, waiting for transfers between devices, body(): lax.all_gather(value_weight, 'fsdp', axis=0, tiled=True)  106 us
    dot_general x1, matrix products, compute_block(): jnp.einsum('wkgrs,wskd->wkgrd', weights.astype(jnp.bfloat16), value_block...  12.9 us
    dot_general x1, local copies, waits for them, and re-layouts, body(): key_proj = jnp.dot(flattened, pieces[0], preferred_element_type=jnp.float32)  12.1 us
    dot_general x1, matrix products, body(): key_proj = jnp.dot(flattened, pieces[0], preferred_element_type=jnp.float32)  7.04 us
    dot_general x1, matrix products, body(): jnp.dot(flattened, pieces[1], preferred_element_type=jnp.float32)  6.98 us
  transfers between devices with their start and end apart: 2, of which 2 were waited for; matrix products, arithmetic and copies ran while one was open for 10% of the time, Pallas kernels for 0%

commit v1 on v0

v1 whole, which is shorter than its diff:
```python
import functools

import jax
import jax.numpy as jnp
import numpy as np
from jax import lax
from jax.experimental import pallas as pl
from jax.experimental.pallas import tpu as pltpu
from jax.sharding import PartitionSpec as P

HEAD_DIM = 128
GROUP = 8
THETA = 500000.0
MASKED = -1e30
MESH = pl.DeviceIdType.MESH
PHASES = 2


def rotary_tables(length):
    half = HEAD_DIM // 2
    exponent = -np.arange(half, dtype=np.float32) * np.float32(2.0) / np.float32(HEAD_DIM)
    frequency = np.power(np.float32(THETA), exponent, dtype=np.float32)
    angles = np.arange(length, dtype=np.float32)[:, None] * frequency[None, :]
    cosine, sine = np.cos(angles).astype(np.float32), np.sin(angles).astype(np.float32)
    return np.concatenate([cosine, cosine], 1), np.concatenate([-sine, sine], 1)


def kernel(
    groups, shards, doc_ref, normed_ref, queries_ref, key_ref, value_ref, cos_hbm, sin_hbm, out_ref,
    wbuf, xbuf, qbuf, obuf, acc, kbuf, vbuf, bias, cos_ref, sin_ref,
    load_sem, recv_sem, z_sem, y_sem, x_sem, pair_send, pair_recv, out_sem, out_send, out_recv,
):
    twins = groups == 2
    ny = 2 if twins else 1
    nz = shards // ny
    parts = 4 if twins else 1
    zparts = 3 if twins else 1
    g, f, c = lax.axis_index("group"), lax.axis_index("fsdp"), lax.axis_index("ctx")
    z, y = f // ny, f % ny
    own_rows, depth = normed_ref.shape[1], key_ref.shape[0]
    length = 2 * own_rows
    piece_rows = depth // parts
    half_cols = queries_ref.shape[2] // 2
    pair = (g, f, 1 - c)
    up, down = (g, f + ny, c), (g, f - ny, c)
    if twins:
        y_dev, x_dev = (g, z * 2 + 1 - y, c), (1 - g, f, c)

    def shard(zs, ys):
        return zs * ny + ys

    def part(j):
        return g * (parts - 1) + j * (1 - 2 * g) if twins else 0

    def piece(h, s, q):
        return wbuf.at[h, s, pl.ds(pl.multiple_of(q * piece_rows, piece_rows), piece_rows), :]

    def copy(h, s, q, send_sem, device):
        ref = piece(h, s, q)
        return pltpu.make_async_remote_copy(
            src_ref=ref, dst_ref=ref, send_sem=send_sem, recv_sem=recv_sem.at[h, s, q],
            device_id=device, device_id_type=MESH,
        )

    def z_copy(h, zs, j, way):
        q = part(j)
        return copy(h, shard(zs, y), q, z_sem.at[way, h, zs, j], up if way == 0 else down)

    def y_copy(h, zs, j):
        return copy(h, shard(zs, y), part(j), y_sem.at[h, zs, j], y_dev)

    def x_copy(h, zs, ys, j, slot):
        return copy(h, shard(zs, ys), part(j), x_sem.at[h, zs, slot], x_dev)

    def wait_piece(h, s, j):
        q = part(j)
        copy(h, s, q, recv_sem.at[h, s, q], pair).wait_recv()

    head_cols = [pl.ds(pl.multiple_of((2 * c + h) * HEAD_DIM, HEAD_DIM), HEAD_DIM) for h in range(PHASES)]
    weight_loads = []
    for h in range(PHASES):
        weight_loads.append([
            pltpu.make_async_copy(key_ref.at[:, head_cols[h]], wbuf.at[h, f, :, pl.ds(0, HEAD_DIM)], load_sem.at[2 * h]),
            pltpu.make_async_copy(value_ref.at[:, head_cols[h]], wbuf.at[h, f, :, pl.ds(HEAD_DIM, HEAD_DIM)], load_sem.at[2 * h + 1]),
        ])
    own = pl.ds(pl.multiple_of(c * own_rows, own_rows), own_rows)
    other = pl.ds(pl.multiple_of((1 - c) * own_rows, own_rows), own_rows)
    my_cols = pl.ds(pl.multiple_of(c * half_cols, half_cols), half_cols)
    other_cols = pl.ds(pl.multiple_of((1 - c) * half_cols, half_cols), half_cols)
    other_loads = [
        pltpu.make_async_copy(normed_ref.at[0], xbuf.at[own, :], load_sem.at[4]),
        pltpu.make_async_copy(queries_ref.at[0, :, my_cols], qbuf.at[own, :], load_sem.at[5]),
        pltpu.make_async_copy(cos_hbm, cos_ref, load_sem.at[6]),
        pltpu.make_async_copy(sin_hbm, sin_ref, load_sem.at[7]),
    ]
    for loads in weight_loads:
        for load in loads:
            load.start()

    barrier = pltpu.get_barrier_semaphore()
    pl.semaphore_signal(barrier, inc=1, device_id=pair, device_id_type=MESH)
    if twins:
        pl.semaphore_signal(barrier, inc=1, device_id=y_dev, device_id_type=MESH)
        pl.semaphore_signal(barrier, inc=1, device_id=x_dev, device_id_type=MESH)

    @pl.when(z < nz - 1)
    def _():
        pl.semaphore_signal(barrier, inc=1, device_id=up, device_id_type=MESH)

    @pl.when(z > 0)
    def _():
        pl.semaphore_signal(barrier, inc=1, device_id=down, device_id_type=MESH)

    line_peers = jnp.where(z > 0, 1, 0) + jnp.where(z < nz - 1, 1, 0)
    pl.semaphore_wait(barrier, (3 if twins else 1) + line_peers)

    def send_own(h):
        for load in weight_loads[h]:
            load.wait()
        for j in range(parts):
            if j < zparts:
                @pl.when(z < nz - 1)
                def _():
                    z_copy(h, z, j, 0).start()

                @pl.when(z > 0)
                def _():
                    z_copy(h, z, j, 1).start()
            if twins:
                y_copy(h, z, j).start()

    def each_way(d, action):
        @pl.when(z - d >= 0)
        def _():
            action(z - d, 0)

        @pl.when(z + d < nz)
        def _():
            action(z + d, 1)

    def passes_on(way):
        return z < nz - 1 if way == 0 else z > 0

    def forward_z(h, d):
        for j in range(zparts):
            def one(zs, way, j=j):
                wait_piece(h, shard(zs, y), j)

                @pl.when(passes_on(way))
                def _():
                    z_copy(h, zs, j, way).start()

                if twins:
                    if j < 2:
                        y_copy(h, zs, j).start()
                    if j == 0:
                        x_copy(h, zs, y, 0, 0).start()

            each_way(d, one)

    def forward_y(h, d):
        for j in range(2):
            def one(zs, way, j=j):
                wait_piece(h, shard(zs, 1 - y), j)
                x_copy(h, zs, 1 - y, j, 1 + j).start()

            each_way(d, one)

    def drain_sends(h, d):
        def one(zs, way):
            for j in range(zparts):
                @pl.when(passes_on(way))
                def _():
                    z_copy(h, zs, j, way).wait_send()

            if twins:
                for j in range(2):
                    y_copy(h, zs, j).wait_send()
                    x_copy(h, zs, 1 - y, j, 1 + j).wait_send()
                x_copy(h, zs, y, 0, 0).wait_send()

        each_way(d, one)

    def drain_own(h):
        for j in range(parts):
            if j < zparts:
                @pl.when(z < nz - 1)
                def _():
                    z_copy(h, z, j, 0).wait_send()

                @pl.when(z > 0)
                def _():
                    z_copy(h, z, j, 1).wait_send()
            if twins:
                y_copy(h, z, j).wait_send()

    def add_shard(h, s):
        columns = pl.ds(pl.multiple_of(s * depth, depth), depth)

        def tile(t, carry):
            rows = pl.ds(pl.multiple_of(t * 256, 256), 256)
            acc[h, rows, :] += jnp.dot(xbuf[rows, columns], wbuf[h, s], preferred_element_type=jnp.float32)
            return carry

        lax.fori_loop(0, length // 256, tile, 0)

    def add_same(h, d):
        def one(zs, way):
            if twins:
                wait_piece(h, shard(zs, y), 3)
            add_shard(h, shard(zs, y))

        each_way(d, one)

    def add_other(h, d):
        def one(zs, way):
            for j in range(2, 4):
                wait_piece(h, shard(zs, 1 - y), j)
            add_shard(h, shard(zs, 1 - y))

        each_way(d, one)

    def add_beside(h):
        for j in range(4):
            wait_piece(h, shard(z, 1 - y), j)
        add_shard(h, shard(z, 1 - y))

    def rotated(u, rows):
        return (u * cos_ref[rows, :] + pltpu.roll(u, HEAD_DIM // 2, 1) * sin_ref[rows, :]).astype(jnp.bfloat16)

    def rotate_queries():
        for load in other_loads[1:]:
            load.wait()
        query_copy.wait_recv()

        def head(i, carry):
            cols = pl.ds(pl.multiple_of(i * HEAD_DIM, HEAD_DIM), HEAD_DIM)

            def tile(t, carry):
                rows = pl.ds(pl.multiple_of(t * 128, 128), 128)
                qbuf[rows, cols] = rotated(qbuf[rows, cols].astype(jnp.float32), rows)
                return carry

            return lax.fori_loop(0, length // 128, tile, carry)

        lax.fori_loop(0, half_cols // HEAD_DIM, head, 0)

    def make_bias():
        first = doc_ref[0]
        row = lax.broadcasted_iota(jnp.int32, (length, length), 0)
        col = lax.broadcasted_iota(jnp.int32, (length, length), 1)
        visible = (col <= row) & ((col >= first) | (row < first))
        bias[...] = jnp.where(visible, 0.0, MASKED)

    def finish_heads(h):
        def tile(t, carry):
            rows = pl.ds(pl.multiple_of(t * 128, 128), 128)
            kbuf[h, rows, :] = rotated(acc[h, rows, :HEAD_DIM], rows)
            vbuf[h, rows, :] = acc[h, rows, HEAD_DIM:].astype(jnp.bfloat16)
            return carry

        lax.fori_loop(0, length // 128, tile, 0)

    factor = HEAD_DIM ** -0.5 * 1.4426950408889634

    def attend(h, first, count):
        def head(i, carry):
            cols = pl.ds(pl.multiple_of((h * GROUP + i) * HEAD_DIM, HEAD_DIM), HEAD_DIM)
            for block in range(2):
                rows = slice(block * own_rows, (block + 1) * own_rows)
                keys = (block + 1) * own_rows
                scores = lax.dot_general(
                    qbuf[rows, cols], kbuf[h, :keys, :], (((1,), (1,)), ((), ())),
                    preferred_element_type=jnp.float32,
                ) * factor + bias[rows, :keys]
                probs = jnp.exp2(scores - jnp.max(scores, axis=1, keepdims=True))
                total = jnp.sum(probs, axis=1, keepdims=True)
                mixed = jnp.dot(probs.astype(jnp.bfloat16), vbuf[h, :keys, :], preferred_element_type=jnp.float32)
                obuf[rows, cols] = (mixed / total).astype(jnp.bfloat16)
            return carry

        lax.fori_loop(first, first + count, head, 0)

    def out_copies(h):
        width = GROUP * HEAD_DIM
        source = pl.ds(h * width, width)
        target = out_ref.at[0, :, pl.ds(pl.multiple_of((2 * c + h) * width, width), width)]
        return (
            pltpu.make_async_copy(obuf.at[own, source], target, out_sem.at[h]),
            pltpu.make_async_remote_copy(
                src_ref=obuf.at[other, source], dst_ref=target, send_sem=out_send.at[h],
                recv_sem=out_recv.at[h], device_id=pair, device_id_type=MESH,
            ),
        )

    def send_out(h):
        for one in out_copies(h):
            one.start()

    send_own(0)
    query_copy = pltpu.make_async_remote_copy(
        src_ref=queries_ref.at[0, :, other_cols], dst_ref=qbuf.at[own, :], send_sem=pair_send.at[0],
        recv_sem=pair_recv.at[0], device_id=pair, device_id_type=MESH,
    )
    normed_copy = pltpu.make_async_remote_copy(
        src_ref=normed_ref.at[0], dst_ref=xbuf.at[own, :], send_sem=pair_send.at[1],
        recv_sem=pair_recv.at[1], device_id=pair, device_id_type=MESH,
    )
    for load in other_loads:
        load.start()
    query_copy.start()
    normed_copy.start()
    acc[...] = jnp.zeros_like(acc)
    make_bias()

    def wait_normed():
        other_loads[0].wait()
        normed_copy.wait_recv()

    if twins:
        forward_z(0, 1)
        rotate_queries()
        forward_z(0, 2)
        forward_y(0, 1)
        send_own(1)
        forward_z(0, 3)
        forward_y(0, 2)
        wait_normed()
        add_shard(0, f)
        add_beside(0)
        add_same(0, 1)
        forward_y(0, 3)
        forward_z(1, 1)
        add_same(0, 2)
        add_other(0, 1)
        forward_z(1, 2)
        forward_y(1, 1)
        add_same(0, 3)
        add_other(0, 2)
        add_other(0, 3)
        finish_heads(0)
        attend(0, 0, 2)
        forward_z(1, 3)
        forward_y(1, 2)
        attend(0, 2, 2)
        add_shard(1, f)
        add_beside(1)
        forward_y(1, 3)
        attend(0, 4, 4)
        send_out(0)
        for d in (1, 2, 3):
            add_same(1, d)
            add_other(1, d)
        finish_heads(1)
    else:
        rotate_queries()
        send_own(1)
        wait_normed()
        for h in range(PHASES):
            add_shard(h, f)

            def step(d, carry, h=h):
                forward_z(h, d)
                add_same(h, d)
                return carry

            lax.fori_loop(1, nz, step, 0)
            finish_heads(h)
            if h == 0:
                attend(0, 0, GROUP)
                send_out(0)
    attend(1, 0, GROUP)
    send_out(1)

    for h in range(PHASES):
        drain_own(h)

        def drain(d, carry, h=h):
            drain_sends(h, d)
            return carry

        lax.fori_loop(1, nz, drain, 0)
    query_copy.wait_send()
    normed_copy.wait_send()
    for h in range(PHASES):
        local, remote = out_copies(h)
        local.wait()
        remote.wait()


def body(groups, shards, normed, queries, key_weight, value_weight, doc_start):
    _, rows, width = normed.shape
    depth = key_weight.shape[0]
    query_cols = queries.shape[2]
    length = 2 * rows
    nz = shards // 2 if groups == 2 else shards
    parts = 4 if groups == 2 else 1
    cosine, sine = rotary_tables(length)
    dma = pltpu.SemaphoreType.DMA
    hbm = pl.BlockSpec(memory_space=pl.ANY)
    return pl.pallas_call(
        functools.partial(kernel, groups, shards),
        out_shape=jax.ShapeDtypeStruct((1, rows, query_cols), jnp.bfloat16),
        in_specs=[pl.BlockSpec(memory_space=pltpu.SMEM)] + [hbm] * 6,
        out_specs=hbm,
        scratch_shapes=[
            pltpu.VMEM((PHASES, shards, depth, 2 * HEAD_DIM), jnp.bfloat16),
            pltpu.VMEM((length, width), jnp.bfloat16),
            pltpu.VMEM((length, query_cols // 2), jnp.bfloat16),
            pltpu.VMEM((length, query_cols // 2), jnp.bfloat16),
            pltpu.VMEM((PHASES, length, 2 * HEAD_DIM), jnp.float32),
            pltpu.VMEM((PHASES, length, HEAD_DIM), jnp.bfloat16),
            pltpu.VMEM((PHASES, length, HEAD_DIM), jnp.bfloat16),
            pltpu.VMEM((length, length), jnp.float32),
            pltpu.VMEM((length, HEAD_DIM), jnp.float32),
            pltpu.VMEM((length, HEAD_DIM), jnp.float32),
            dma((8,)),
            dma((PHASES, shards, parts)),
            dma((2, PHASES, nz, 3)),
            dma((PHASES, nz, 4)),
            dma((PHASES, nz, 3)),
            dma((2,)),
            dma((2,)),
            dma((2,)),
            dma((2,)),
            dma((2,)),
        ],
        compiler_params=pltpu.CompilerParams(
            collective_id=0, has_side_effects=True, vmem_limit_bytes=56 * 1024 * 1024
        ),
    )(doc_start, normed, queries, key_weight, value_weight, jnp.asarray(cosine), jnp.asarray(sine))


def solution(mesh):
    placed = (
        P(("group", "fsdp"), "ctx", None),
        P(("group", "fsdp"), "ctx", None),
        P("fsdp", None),
        P("fsdp", None),
        P(("group", "fsdp")),
    )
    return jax.shard_map(
        functools.partial(body, mesh.shape["group"], mesh.shape["fsdp"]),
        mesh=mesh,
        in_specs=placed,
        out_specs=P(("group", "fsdp"), "ctx", None),
        check_vma=False,
    )
```

time: 314 us -> 89.1 us (0.28)
  waiting for transfers between devices: 224 us -> 0 us
  Pallas kernels: 0 us -> 85.2 us
  matrix products: 29.7 us -> 0 us
  local copies, waits for them, and re-layouts: 24 us -> 3.13 us
  other arithmetic: 17.7 us -> 0 us
  between operations: 14.2 us -> 0.66 us
  blocking collectives: 4.35 us -> 0 us
    all_gather x2 -> x0, waiting for transfers between devices: 222 us -> none  [the longest x1 116 us: body(): lax.all_gather(key_weight, 'fsdp', axis=0, tiled=True)]
    pallas_call x0 -> x1, Pallas kernels: none -> 85.2 us  [body(): pl.pallas_call(functools.partial(kernel, groups, shards), out_shape=jax.S...]
    dot_general x4 -> x0, matrix products: 29.7 us -> none  [the longest x1 12.9 us: compute_block(): jnp.einsum('wkgrs,wskd->wkgrd', weights.astype(jnp.bfloat16), value_block...]
    dot_general x1 -> x0, local copies, waits for them, and re-layouts: 12.1 us -> none  [body(): key_proj = jnp.dot(flattened, pieces[0], preferred_element_type=jnp.float32)]
    cond x2 -> x0, local copies, waits for them, and re-layouts: 5.71 us -> none
    another operation x3 -> x0, other arithmetic: 4.99 us -> none
    all_gather x2 -> x0, blocking collectives: 4.35 us -> none  [the longest x1 2.18 us: body(): lax.all_gather(key_heads, 'ctx', axis=1, tiled=True)]
    reduce_sum x1 -> x0, other arithmetic: 4.18 us -> none  [compute_block(): denominator = jnp.sum(weights, axis=-1)]
  transfers between devices with their start and end apart: 2 -> 0, of which waited for: 2 -> 0; matrix products, arithmetic and copies ran while one was open for 10% -> 0% of each run, Pallas kernels for 0% -> 0%
where the time goes in v1:
time: 89.1 us; the launch traced here: 89 us
  Pallas kernels  85.2 us (96%)
  local copies, waits for them, and re-layouts  3.13 us (4%)
    pallas_call x1, Pallas kernels, body(): pl.pallas_call(functools.partial(kernel, groups, shards), out_shape=jax.S...  85.2 us
    unnamed x1, local copies, waits for them, and re-layouts  3.13 us

profile of v1, /device:TPU:0, one launch (start us, length us, event | category | flops | bytes accessed | tf_op | source)
XLA Modules:
  0.0 89.0 jit_solution(7301399293302006094)
XLA Ops:
  0.7 85.2 %shard_map.73 = bf16[1,256,4096]{2,1,0:T(8,128)(2,1)} custom-call(s32[1]{0:T(128)S(6)} %copy.9.doc_ref, bf16[1,256,8192]{2,1,0:T(8,128)(2,1)} %normed_ref.1, bf16[1,256,4096]{2,1,0:T(8,128)(2,1)} %queries_ref.1, bf16[1024,512]{1,0:T(8,128)(2,1)} %key_ref.1, bf16[1024,512]{1,0:T(8,128)(2,1)} %value_ref.1, f32[512,128]{1,0:T(8,128)} %constant.4.clone.cos_hbm, ...), custom_call_target="tpu_custom_call" | custom-call | tf_op jit(solution)/shard_map/pallas_call | solution.py:401
  85.9 3.1 %copy.10 = bf16[1,256,4096]{2,1,0:T(8,128)(2,1)} copy(bf16[1,256,4096]{2,1,0:T(8,128)(2,1)} %shard_map.73) | data formatting | bytes 4194304

commit v2 on v1

--- a/solution.py
+++ b/solution.py
@@ -14,6 +14,7 @@
 MASKED = -1e30
 MESH = pl.DeviceIdType.MESH
 PHASES = 2
+OUT_GROUPS = 4
 
 
 def rotary_tables(length):
@@ -27,7 +28,7 @@
 
 def kernel(
     groups, shards, doc_ref, normed_ref, queries_ref, key_ref, value_ref, cos_hbm, sin_hbm, out_ref,
-    wbuf, xbuf, qbuf, obuf, acc, kbuf, vbuf, bias, cos_ref, sin_ref,
+    wbuf, xbuf, qbuf, obuf, pbuf, inverse, acc, kbuf, vbuf, bias, cos_ref, sin_ref,
     load_sem, recv_sem, z_sem, y_sem, x_sem, pair_send, pair_recv, out_sem, out_send, out_recv,
 ):
     twins = groups == 2
@@ -76,26 +77,23 @@
         q = part(j)
         copy(h, s, q, recv_sem.at[h, s, q], pair).wait_recv()
 
-    head_cols = [pl.ds(pl.multiple_of((2 * c + h) * HEAD_DIM, HEAD_DIM), HEAD_DIM) for h in range(PHASES)]
-    weight_loads = []
-    for h in range(PHASES):
-        weight_loads.append([
-            pltpu.make_async_copy(key_ref.at[:, head_cols[h]], wbuf.at[h, f, :, pl.ds(0, HEAD_DIM)], load_sem.at[2 * h]),
-            pltpu.make_async_copy(value_ref.at[:, head_cols[h]], wbuf.at[h, f, :, pl.ds(HEAD_DIM, HEAD_DIM)], load_sem.at[2 * h + 1]),
-        ])
+    head_cols = pl.ds(pl.multiple_of(c * 2 * HEAD_DIM, 2 * HEAD_DIM), 2 * HEAD_DIM)
+    weight_loads = [
+        pltpu.make_async_copy(ref.at[:, head_cols], wbuf.at[h, f], load_sem.at[h])
+        for h, ref in enumerate((key_ref, value_ref))
+    ]
     own = pl.ds(pl.multiple_of(c * own_rows, own_rows), own_rows)
     other = pl.ds(pl.multiple_of((1 - c) * own_rows, own_rows), own_rows)
     my_cols = pl.ds(pl.multiple_of(c * half_cols, half_cols), half_cols)
     other_cols = pl.ds(pl.multiple_of((1 - c) * half_cols, half_cols), half_cols)
     other_loads = [
-        pltpu.make_async_copy(normed_ref.at[0], xbuf.at[own, :], load_sem.at[4]),
-        pltpu.make_async_copy(queries_ref.at[0, :, my_cols], qbuf.at[own, :], load_sem.at[5]),
-        pltpu.make_async_copy(cos_hbm, cos_ref, load_sem.at[6]),
-        pltpu.make_async_copy(sin_hbm, sin_ref, load_sem.at[7]),
+        pltpu.make_async_copy(normed_ref.at[0], xbuf.at[own, :], load_sem.at[2]),
+        pltpu.make_async_copy(queries_ref.at[0, :, my_cols], qbuf.at[own, :], load_sem.at[3]),
+        pltpu.make_async_copy(cos_hbm, cos_ref, load_sem.at[4]),
+        pltpu.make_async_copy(sin_hbm, sin_ref, load_sem.at[5]),
     ]
-    for loads in weight_loads:
-        for load in loads:
-            load.start()
+    for load in weight_loads:
+        load.start()
 
     barrier = pltpu.get_barrier_semaphore()
     pl.semaphore_signal(barrier, inc=1, device_id=pair, device_id_type=MESH)
@@ -114,9 +112,11 @@
     line_peers = jnp.where(z > 0, 1, 0) + jnp.where(z < nz - 1, 1, 0)
     pl.semaphore_wait(barrier, (3 if twins else 1) + line_peers)
 
+    def sends_beside(h, j):
+        return twins and (h != 0 or j != 3)
+
     def send_own(h):
-        for load in weight_loads[h]:
-            load.wait()
+        weight_loads[h].wait()
         for j in range(parts):
             if j < zparts:
                 @pl.when(z < nz - 1)
@@ -126,7 +126,7 @@
                 @pl.when(z > 0)
                 def _():
                     z_copy(h, z, j, 1).start()
-            if twins:
+            if sends_beside(h, j):
                 y_copy(h, z, j).start()
 
     def each_way(d, action):
@@ -191,8 +191,10 @@
                 @pl.when(z > 0)
                 def _():
                     z_copy(h, z, j, 1).wait_send()
-            if twins:
+            if sends_beside(h, j):
                 y_copy(h, z, j).wait_send()
+        if twins and h == 0:
+            x_copy(h, z, 1 - y, 0, 0).wait_send()
 
     def add_shard(h, s):
         columns = pl.ds(pl.multiple_of(s * depth, depth), depth)
@@ -220,8 +222,12 @@
 
         each_way(d, one)
 
+    def forward_beside():
+        wait_piece(0, shard(z, 1 - y), 0)
+        x_copy(0, z, 1 - y, 0, 0).start()
+
     def add_beside(h):
-        for j in range(4):
+        for j in range(1 if h == 0 else 0, 4):
             wait_piece(h, shard(z, 1 - y), j)
         add_shard(h, shard(z, 1 - y))
 
@@ -252,20 +258,22 @@
         visible = (col <= row) & ((col >= first) | (row < first))
         bias[...] = jnp.where(visible, 0.0, MASKED)
 
-    def finish_heads(h):
+    def finish_keys():
         def tile(t, carry):
             rows = pl.ds(pl.multiple_of(t * 128, 128), 128)
-            kbuf[h, rows, :] = rotated(acc[h, rows, :HEAD_DIM], rows)
-            vbuf[h, rows, :] = acc[h, rows, HEAD_DIM:].astype(jnp.bfloat16)
+            for h in range(2):
+                kbuf[h, rows, :] = rotated(acc[0, rows, h * HEAD_DIM:(h + 1) * HEAD_DIM], rows)
             return carry
 
         lax.fori_loop(0, length // 128, tile, 0)
 
     factor = HEAD_DIM ** -0.5 * 1.4426950408889634
 
-    def attend(h, first, count):
+    def weigh(first, count):
+        h = first // GROUP
+
         def head(i, carry):
-            cols = pl.ds(pl.multiple_of((h * GROUP + i) * HEAD_DIM, HEAD_DIM), HEAD_DIM)
+            cols = pl.ds(pl.multiple_of(i * HEAD_DIM, HEAD_DIM), HEAD_DIM)
             for block in range(2):
                 rows = slice(block * own_rows, (block + 1) * own_rows)
                 keys = (block + 1) * own_rows
@@ -275,16 +283,33 @@
                 ) * factor + bias[rows, :keys]
                 probs = jnp.exp2(scores - jnp.max(scores, axis=1, keepdims=True))
                 total = jnp.sum(probs, axis=1, keepdims=True)
-                mixed = jnp.dot(probs.astype(jnp.bfloat16), vbuf[h, :keys, :], preferred_element_type=jnp.float32)
-                obuf[rows, cols] = (mixed / total).astype(jnp.bfloat16)
+                pbuf[i, rows, :keys] = probs.astype(jnp.bfloat16)
+                inverse[i, rows, :] = jnp.broadcast_to(1.0 / total, (own_rows, HEAD_DIM))
             return carry
 
         lax.fori_loop(first, first + count, head, 0)
 
+    def mix(first, count):
+        h = first // GROUP
+
+        def head(i, carry):
+            cols = pl.ds(pl.multiple_of(i * HEAD_DIM, HEAD_DIM), HEAD_DIM)
+            for block in range(2):
+                rows = slice(block * own_rows, (block + 1) * own_rows)
+                keys = (block + 1) * own_rows
+                mixed = jnp.dot(
+                    pbuf[i, rows, :keys], vbuf[:keys, h * HEAD_DIM:(h + 1) * HEAD_DIM],
+                    preferred_element_type=jnp.float32,
+                )
+                obuf[rows, cols] = (mixed * inverse[i, rows, :]).astype(jnp.bfloat16)
+            return carry
+
+        lax.fori_loop(first, first + count, head, 0)
+
     def out_copies(h):
-        width = GROUP * HEAD_DIM
+        width = half_cols // OUT_GROUPS
         source = pl.ds(h * width, width)
-        target = out_ref.at[0, :, pl.ds(pl.multiple_of((2 * c + h) * width, width), width)]
+        target = out_ref.at[0, :, pl.ds(pl.multiple_of(c * half_cols + h * width, width), width)]
         return (
             pltpu.make_async_copy(obuf.at[own, source], target, out_sem.at[h]),
             pltpu.make_async_remote_copy(
@@ -320,38 +345,40 @@
     if twins:
         forward_z(0, 1)
         rotate_queries()
+        forward_beside()
         forward_z(0, 2)
         forward_y(0, 1)
         send_own(1)
+        forward_y(0, 2)
         forward_z(0, 3)
-        forward_y(0, 2)
         wait_normed()
         add_shard(0, f)
         add_beside(0)
         add_same(0, 1)
         forward_y(0, 3)
-        forward_z(1, 1)
         add_same(0, 2)
         add_other(0, 1)
-        forward_z(1, 2)
-        forward_y(1, 1)
+        forward_z(1, 1)
         add_same(0, 3)
         add_other(0, 2)
         add_other(0, 3)
-        finish_heads(0)
-        attend(0, 0, 2)
+        finish_keys()
+        weigh(0, 2)
+        forward_z(1, 2)
+        weigh(2, 2)
+        forward_y(1, 1)
+        weigh(4, 2)
+        add_shard(1, f)
+        forward_y(1, 2)
+        weigh(6, 2)
         forward_z(1, 3)
-        forward_y(1, 2)
-        attend(0, 2, 2)
-        add_shard(1, f)
+        weigh(8, 2)
+        forward_y(1, 3)
+        weigh(10, 6)
         add_beside(1)
-        forward_y(1, 3)
-        attend(0, 4, 4)
-        send_out(0)
         for d in (1, 2, 3):
             add_same(1, d)
             add_other(1, d)
-        finish_heads(1)
     else:
         rotate_queries()
         send_own(1)
@@ -365,12 +392,15 @@
                 return carry
 
             lax.fori_loop(1, nz, step, 0)
-            finish_heads(h)
             if h == 0:
-                attend(0, 0, GROUP)
-                send_out(0)
-    attend(1, 0, GROUP)
-    send_out(1)
+                finish_keys()
+                weigh(0, 8)
+                weigh(8, 8)
+    vbuf[...] = acc[1].astype(jnp.bfloat16)
+    heads = 2 * GROUP // OUT_GROUPS
+    for group in range(OUT_GROUPS):
+        mix(group * heads, heads)
+        send_out(group)
 
     for h in range(PHASES):
         drain_own(h)
@@ -382,8 +412,8 @@
         lax.fori_loop(1, nz, drain, 0)
     query_copy.wait_send()
     normed_copy.wait_send()
-    for h in range(PHASES):
-        local, remote = out_copies(h)
+    for group in range(OUT_GROUPS):
+        local, remote = out_copies(group)
         local.wait()
         remote.wait()
 
@@ -408,22 +438,24 @@
             pltpu.VMEM((length, width), jnp.bfloat16),
             pltpu.VMEM((length, query_cols // 2), jnp.bfloat16),
             pltpu.VMEM((length, query_cols // 2), jnp.bfloat16),
+            pltpu.VMEM((2 * GROUP, length, length), jnp.bfloat16),
+            pltpu.VMEM((2 * GROUP, length, HEAD_DIM), jnp.float32),
             pltpu.VMEM((PHASES, length, 2 * HEAD_DIM), jnp.float32),
-            pltpu.VMEM((PHASES, length, HEAD_DIM), jnp.bfloat16),
-            pltpu.VMEM((PHASES, length, HEAD_DIM), jnp.bfloat16),
+            pltpu.VMEM((2, length, HEAD_DIM), jnp.bfloat16),
+            pltpu.VMEM((length, 2 * HEAD_DIM), jnp.bfloat16),
             pltpu.VMEM((length, length), jnp.float32),
             pltpu.VMEM((length, HEAD_DIM), jnp.float32),
             pltpu.VMEM((length, HEAD_DIM), jnp.float32),
-            dma((8,)),
+            dma((6,)),
             dma((PHASES, shards, parts)),
             dma((2, PHASES, nz, 3)),
             dma((PHASES, nz, 4)),
             dma((PHASES, nz, 3)),
             dma((2,)),
             dma((2,)),
-            dma((2,)),
-            dma((2,)),
-            dma((2,)),
+            dma((OUT_GROUPS,)),
+            dma((OUT_GROUPS,)),
+            dma((OUT_GROUPS,)),
         ],
         compiler_params=pltpu.CompilerParams(
             collective_id=0, has_side_effects=True, vmem_limit_bytes=56 * 1024 * 1024

time: 89.1 us -> 83.8 us (0.941)
  Pallas kernels: 85.2 us -> 79.8 us
    pallas_call x1, Pallas kernels: 85.2 us -> 79.8 us  [body(): pl.pallas_call(functools.partial(kernel, groups, shards), out_shape=jax.S...]
where the time goes in v2:
time: 83.8 us; the launch traced here: 83.6 us
  Pallas kernels  79.8 us (95%)
  local copies, waits for them, and re-layouts  3.13 us (4%)
    pallas_call x1, Pallas kernels, body(): pl.pallas_call(functools.partial(kernel, groups, shards), out_shape=jax.S...  79.8 us
    unnamed x1, local copies, waits for them, and re-layouts  3.13 us

profile of v2, /device:TPU:0, one launch (start us, length us, event | category | flops | bytes accessed | tf_op | source)
XLA Modules:
  0.0 83.6 jit_solution(1778620570320763064)
XLA Ops:
  0.7 79.8 %shard_map.73 = bf16[1,256,4096]{2,1,0:T(8,128)(2,1)} custom-call(s32[1]{0:T(128)S(6)} %copy.9.doc_ref, bf16[1,256,8192]{2,1,0:T(8,128)(2,1)} %normed_ref.1, bf16[1,256,4096]{2,1,0:T(8,128)(2,1)} %queries_ref.1, bf16[1024,512]{1,0:T(8,128)(2,1)} %key_ref.1, bf16[1024,512]{1,0:T(8,128)(2,1)} %value_ref.1, f32[512,128]{1,0:T(8,128)} %constant.4.clone.cos_hbm, ...), custom_call_target="tpu_custom_call" | custom-call | tf_op jit(solution)/shard_map/pallas_call | solution.py:431
  80.5 3.1 %copy.10 = bf16[1,256,4096]{2,1,0:T(8,128)(2,1)} copy(bf16[1,256,4096]{2,1,0:T(8,128)(2,1)} %shard_map.73) | data formatting | bytes 4194304

commit v3 on v2

--- a/solution.py
+++ b/solution.py
@@ -141,8 +141,8 @@
     def passes_on(way):
         return z < nz - 1 if way == 0 else z > 0
 
-    def forward_z(h, d):
-        for j in range(zparts):
+    def forward_z(h, d, some=None):
+        for j in range(zparts) if some is None else some:
             def one(zs, way, j=j):
                 wait_piece(h, shard(zs, y), j)
 
@@ -364,21 +364,31 @@
         add_other(0, 3)
         finish_keys()
         weigh(0, 2)
-        forward_z(1, 2)
+        forward_z(1, 2, [0])
         weigh(2, 2)
+        forward_z(1, 2, [1])
+        weigh(4, 2)
+        forward_z(1, 2, [2])
+        weigh(6, 2)
         forward_y(1, 1)
-        weigh(4, 2)
         add_shard(1, f)
+        add_beside(1)
+        weigh(8, 1)
+        forward_z(1, 3, [0])
+        weigh(9, 2)
+        add_same(1, 1)
+        forward_z(1, 3, [1])
+        weigh(11, 2)
+        add_other(1, 1)
         forward_y(1, 2)
-        weigh(6, 2)
-        forward_z(1, 3)
-        weigh(8, 2)
+        forward_z(1, 3, [2])
+        weigh(13, 2)
+        add_same(1, 2)
         forward_y(1, 3)
-        weigh(10, 6)
-        add_beside(1)
-        for d in (1, 2, 3):
-            add_same(1, d)
-            add_other(1, d)
+        weigh(15, 1)
+        add_other(1, 2)
+        add_same(1, 3)
+        add_other(1, 3)
     else:
         rotate_queries()
         send_own(1)
@@ -427,12 +437,12 @@
     parts = 4 if groups == 2 else 1
     cosine, sine = rotary_tables(length)
     dma = pltpu.SemaphoreType.DMA
-    hbm = pl.BlockSpec(memory_space=pl.ANY)
+    hbm = pl.BlockSpec(memory_space=pltpu.HBM)
     return pl.pallas_call(
         functools.partial(kernel, groups, shards),
         out_shape=jax.ShapeDtypeStruct((1, rows, query_cols), jnp.bfloat16),
         in_specs=[pl.BlockSpec(memory_space=pltpu.SMEM)] + [hbm] * 6,
-        out_specs=hbm,
+        out_specs=pl.BlockSpec(memory_space=pl.ANY),
         scratch_shapes=[
             pltpu.VMEM((PHASES, shards, depth, 2 * HEAD_DIM), jnp.bfloat16),
             pltpu.VMEM((length, width), jnp.bfloat16),
@@ -458,7 +468,7 @@
             dma((OUT_GROUPS,)),
         ],
         compiler_params=pltpu.CompilerParams(
-            collective_id=0, has_side_effects=True, vmem_limit_bytes=56 * 1024 * 1024
+            collective_id=0, has_side_effects=True, vmem_limit_bytes=48 * 1024 * 1024
         ),
     )(doc_start, normed, queries, key_weight, value_weight, jnp.asarray(cosine), jnp.asarray(sine))
 

time: 83.8 us -> 86.4 us (1.031)
  local copies, waits for them, and re-layouts: 3.13 us -> 5.66 us
    unnamed x1 -> x9, local copies, waits for them, and re-layouts: 3.13 us -> 5.66 us
where the time goes in v3:
time: 86.4 us; the launch traced here: 86.1 us
  Pallas kernels  79.8 us (92%)
  local copies, waits for them, and re-layouts  5.66 us (7%)
    pallas_call x1, Pallas kernels, body(): pl.pallas_call(functools.partial(kernel, groups, shards), out_shape=jax.S...  79.8 us
    unnamed x9, local copies, waits for them, and re-layouts  5.66 us

profile of v3, /device:TPU:0, one launch (start us, length us, event | category | flops | bytes accessed | tf_op | source)
XLA Modules:
  0.0 86.1 jit_solution(10777318944097103730)
XLA Ops:
  0.7 0.0 copy-start
  0.7 1.2 %copy-done = bf16[1024,512]{1,0:T(8,128)(2,1)S(1)} copy-done((bf16[1024,512]{1,0:T(8,128)(2,1)S(1)}, bf16[1024,512]{1,0:T(8,128)(2,1)}, u32[]{:S(2)}) %copy-start) | copy-done | bytes 1048600
  1.9 0.0 copy-start.1
  1.9 1.2 %copy-done.1 = bf16[1024,512]{1,0:T(8,128)(2,1)S(1)} copy-done((bf16[1024,512]{1,0:T(8,128)(2,1)S(1)}, bf16[1024,512]{1,0:T(8,128)(2,1)}, u32[]{:S(2)}) %copy-start.1) | copy-done | bytes 1048600
  3.1 0.0 copy-start.2
  3.1 0.9 %copy-done.2 = f32[512,128]{1,0:T(8,128)S(1)} copy-done((f32[512,128]{1,0:T(8,128)S(1)}, f32[512,128]{1,0:T(8,128)}, u32[]{:S(2)}) %copy-start.2) | copy-done | bytes 262168
  4.1 0.0 copy-start.3
  4.1 0.9 %copy-done.3 = f32[512,128]{1,0:T(8,128)S(1)} copy-done((f32[512,128]{1,0:T(8,128)S(1)}, f32[512,128]{1,0:T(8,128)}, u32[]{:S(2)}) %copy-start.3) | copy-done | bytes 262168
  5.0 79.8 %shard_map.73 = bf16[1,256,4096]{2,1,0:T(8,128)(2,1)S(1)} custom-call(s32[1]{0:T(128)S(6)} %copy.9.doc_ref, bf16[1,256,8192]{2,1,0:T(8,128)(2,1)} %normed_ref.1, bf16[1,256,4096]{2,1,0:T(8,128)(2,1)} %queries_ref.1, bf16[1024,512]{1,0:T(8,128)(2,1)S(1)} %copy-done, bf16[1024,512]{1,0:T(8,128)(2,1)S(1)} %copy-done.1, f32[512,128]{1,0:T(8,128)S(1)} %copy-done.3, ...), custom_call_target="tpu_custom_call" | custom-call | tf_op jit(solution)/shard_map/pallas_call | solution.py:441
  84.8 1.3 %copy.10 = bf16[1,256,4096]{2,1,0:T(8,128)(2,1)} copy(bf16[1,256,4096]{2,1,0:T(8,128)(2,1)S(1)} %shard_map.73) | data formatting | bytes 4194304
Async XLA Ops:
  0.7 1.2 %copy-start = (bf16[1024,512]{1,0:T(8,128)(2,1)S(1)}, bf16[1024,512]{1,0:T(8,128)(2,1)}, u32[]{:S(2)}) copy-start(bf16[1024,512]{1,0:T(8,128)(2,1)} %key_ref.1) | copy-start | bytes 3145732
  1.9 1.2 %copy-start.1 = (bf16[1024,512]{1,0:T(8,128)(2,1)S(1)}, bf16[1024,512]{1,0:T(8,128)(2,1)}, u32[]{:S(2)}) copy-start(bf16[1024,512]{1,0:T(8,128)(2,1)} %value_ref.1) | copy-start | bytes 3145732
  3.1 0.9 %copy-start.2 = (f32[512,128]{1,0:T(8,128)S(1)}, f32[512,128]{1,0:T(8,128)}, u32[]{:S(2)}) copy-start(f32[512,128]{1,0:T(8,128)} %constant.5.clone.sin_hbm) | copy-start | bytes 786436
  4.1 0.9 %copy-start.3 = (f32[512,128]{1,0:T(8,128)S(1)}, f32[512,128]{1,0:T(8,128)}, u32[]{:S(2)}) copy-start(f32[512,128]{1,0:T(8,128)} %constant.4.clone.cos_hbm) | copy-start | bytes 786436
